TPU v7x, 128 devices: a whole 4x4x4 slice. The times are simulated.
128 devices in a mesh: req: 16 (over y, z), mdl: 8 (over x, core).
Axes of the slice: x: 4, y: 4, z: 4, core: 2. Of those that a mesh axis runs over, the one named last changes fastest.
Arguments:
- segments: int32 [1024], P('req'), may hold values from -1 to 1023, as said below
- queries: bfloat16 [1024, 8192], P('req', 'mdl'), may hold values from -200 to 200
- keys_values: bfloat16 [1024, 2, 1024], P('req', None, 'mdl'), may hold values from -6 to 6
- page_table: int32 [64], replicated, may hold values from 0 to 127, as said below
- paged_cache: bfloat16 [128, 16, 2, 1024], P('req', None, None, 'mdl'), may hold values from -6 to 6
- residual: bfloat16 [1024, 8192], P(None, 'req'), may hold values from -40 to 40
- out_weight: bfloat16 [8192, 8192], P('mdl', 'req'), may hold values from -0.0625 to 0.0625
- norm_gain: bfloat16 [8192], P('req'), may hold values from 0.099609375 to 1.8984375
- gate_up_weight: bfloat16 [8192, 2, 29568], P('req', None, 'mdl'), may hold values from -0.0625 to 0.0625
Outputs:
- hidden: bfloat16 [1024, 29568], P('req', 'mdl')
- cache_new: bfloat16 [128, 16, 2, 1024], P('req', None, None, 'mdl')
Inputs may be any that keep to these rules, and one draw needn't show every extreme that they name: `segments`: each block of 64 slots of one index of req holds whole requests followed by pads; a live slot's entry is the slot index of its request's first slot, in that block; in every draw some block has no pads. `page_table`: all entries differ; page p lies on index p // 8 of req; the pages of one block of 64 slots all lie on one index of req, and different blocks on different indices.
All inputs are finite; a program needn't handle non-finite values.
Results may differ from a plain program's by a relative error of at most 0.024.
Values may be sent and summed in bfloat16 or wider, within the bound.
A program may use at most 128 MiB of HBM per device.

v0:
```python
import jax
import jax.numpy as jnp
from jax import lax
from jax.sharding import PartitionSpec as P

D = 8192
HD = 128
QPK = 8
PAGE = 16


EPSILON = 1e-06


def attention_block(query_rows, pair_rows, seg_rows):
    slots = seg_rows.shape[0]
    groups = pair_rows.shape[2] // HD
    query = query_rows.reshape(slots, groups, QPK, HD)
    keys = pair_rows[:, 0].reshape(slots, groups, HD)
    values = pair_rows[:, 1].reshape(slots, groups, HD)
    scores = jnp.einsum("igqd,jgd->gqij", query, keys, preferred_element_type=jnp.float32) * HD ** (
        -0.5
    )
    places = jnp.arange(slots, dtype=jnp.int32)
    allowed = (
        (seg_rows[:, None] == seg_rows[None, :])
        & (seg_rows[:, None] >= 0)
        & (places[None, :] < places[:, None])
    )
    allowed = allowed | (places[:, None] == places[None, :])
    scores = jnp.where(allowed, scores, -jnp.inf)
    highest = jnp.max(scores, axis=-1, keepdims=True)
    weights = jnp.exp(scores - highest)
    probs = (weights / jnp.sum(weights, axis=-1, keepdims=True)).astype(jnp.bfloat16)
    mixed = jnp.einsum("gqij,jgd->igqd", probs, values, preferred_element_type=jnp.float32)
    mixed = jnp.where((seg_rows >= 0)[:, None, None, None], mixed, 0.0)
    return mixed.reshape(slots, groups * QPK * HD).astype(jnp.bfloat16)


def on_device(
    segments,
    queries,
    keys_values,
    page_table,
    paged_cache,
    residual,
    out_weight,
    norm_gain,
    gate_up_weight,
):
    attended = attention_block(queries, keys_values, segments)
    live_rows = (segments >= 0).astype(jnp.bfloat16)
    every_pair, every_live = (
        lax.all_gather(keys_values, "req", axis=0, tiled=True),
        lax.all_gather(live_rows, "req", axis=0, tiled=True),
    )
    local_pages = paged_cache.shape[0]
    slot_count = every_pair.shape[0]
    token_pages = jnp.repeat(page_table, PAGE, total_repeat_length=slot_count)
    target = token_pages - lax.axis_index("req") * local_pages
    writable = (target >= 0) & (target < local_pages) & (every_live > 0)
    target = jnp.where(writable, target, local_pages)
    offsets = jnp.arange(slot_count, dtype=jnp.int32) % PAGE
    cache_new = paged_cache.at[target, offsets].set(every_pair, mode="drop")
    partial_value = jnp.dot(
        lax.all_gather(attended, "req", axis=0, tiled=True),
        out_weight,
        preferred_element_type=jnp.float32,
    )
    gain_row = norm_gain.astype(jnp.float32)
    stream = residual.astype(jnp.float32) + lax.psum(
        partial_value.astype(jnp.bfloat16), "mdl"
    ).astype(jnp.float32)
    squares = jnp.sum(stream * stream, axis=1)
    totals = lax.psum(squares, "req")
    normed = (stream * lax.rsqrt(totals / D + EPSILON)[:, None] * gain_row[None, :]).astype(
        jnp.bfloat16
    )
    flat_weight = gate_up_weight.reshape(gate_up_weight.shape[0], -1)
    summed = lax.psum_scatter(
        jnp.dot(normed, flat_weight, preferred_element_type=jnp.float32).astype(jnp.bfloat16),
        "req",
        scatter_dimension=0,
        tiled=True,
    ).astype(jnp.float32)
    split_at = summed.shape[1] // 2
    hidden = (jax.nn.silu(summed[:, :split_at]) * summed[:, split_at:]).astype(jnp.bfloat16)
    return (hidden, cache_new)


def solution(mesh):
    placed = (
        P("req"),
        P("req", "mdl"),
        P("req", None, "mdl"),
        P(),
        P("req", None, None, "mdl"),
        P(None, "req"),
        P("mdl", "req"),
        P("req"),
        P("req", None, "mdl"),
    )
    return jax.shard_map(
        on_device,
        mesh=mesh,
        in_specs=placed,
        out_specs=(P("req", "mdl"), P("req", None, None, "mdl")),
        check_vma=False,
    )
```

profile of v0, /device:TPU:0, one launch (start us, length us, event | category | flops | bytes accessed | tf_op | source)
XLA Modules:
  0.0 327.6 jit_solution(5003735953313754061)
XLA Ops:
  7.2 0.9 fusion.16
  8.1 0.7 fusion.15
  8.8 0.8 fusion.13
  9.6 1.2 fusion.21
  11.2 0.7 copy.43
  12.0 47.6 %all-gather.2.cloned.1.call-done = bf16[1024,1024]{1,0:T(8,128)(2,1)} async-done(((bf16[64,1024]{1,0:T(8,128)(2,1)}), bf16[1024,1024]{1,0:T(8,128)(2,1)}) %all-gather.2.cloned.1.call-update) | async-done | bytes 2097168 | tf_op jit(solution)/shard_map/all_gather | solution.py:66
  59.6 3.8 %convolution_convert_fusion.1 = bf16[1024,512]{1,0:T(8,128)(2,1)} fusion(bf16[1024,1024]{1,0:T(8,128)(2,1)} %all-gather.2.cloned.1.call-done, bf16[1024,512]{1,0:T(8,128)(2,1)S(1)} %copy-done), kind=kOutput, calls=%fused_computation.5 | convolution fusion | flops 1074266112 | bytes 4194304 | tf_op jit(solution)/shard_map/dot_general | solution.py:65
  63.5 61.8 %all-reduce.3.cloned.1.call-done = bf16[1024,512]{1,0:T(8,128)(2,1)} async-done(((bf16[1024,512]{1,0:T(8,128)(2,1)}), bf16[1024,512]{1,0:T(8,128)(2,1)}) %all-reduce.3.cloned.1.call-update) | async-done | bytes 1048592 | tf_op jit(solution)/shard_map/psum | solution.py:71
  125.3 1.7 multiply_reduce_fusion
  127.1 40.6 %psum.15 = f32[1024]{0:T(1024)S(1)} all-reduce(f32[1024]{0:T(1024)S(1)} %multiply_reduce_fusion), channel_id=1, replica_groups=mesh['req'=16,'mdl'=8] {'req'}, use_global_device_ids=true, to_apply=%region_4.5 | all-reduce | flops 1024 | bytes 8192 | tf_op jit(solution)/shard_map/psum | solution.py:75
  167.7 14.8 %convolution_convert_fusion = bf16[1024,7392]{1,0:T(8,128)(2,1)} fusion(bf16[512,7392]{0,1:T(8,128)(2,1)} %bitcast.142, bf16[1024,512]{1,0:T(8,128)(2,1)S(1)} %copy-done.5, bf16[1024,512]{1,0:T(8,128)(2,1)S(1)} %copy-done.4, f32[512]{0:T(512)S(1)} %convert_element_type.46, f32[1024]{0:T(1024)S(1)} %add_rsqrt_fusion), kind=kOutput, calls=%fused_computation.1 | convolution fusion | flops 7761788928 | bytes 24811520 | tf_op jit(solution)/shard_map/dot_general | solution.py:81
  183.1 0.6 dynamic-slice.6
  184.5 36.8 %all-reduce = bf16[1024]{0:T(1024)(128)(2,1)S(1)} all-reduce(bf16[1024]{0:T(1024)(128)(2,1)S(1)} %dynamic-update-slice.3), channel_id=1, replica_groups=mesh['req'=16,'mdl'=8] {'req'}, use_global_device_ids=true, to_apply=%add | all-reduce | flops 1024 | bytes 4096
  221.3 0.7 fusion.20
  222.0 0.7 fusion.19
  222.7 0.7 fusion.17
  223.4 0.7 fusion.18
  224.3 4.4 %compare_select_fusion.2 = (s32[1024,1]{0,1:T(1,128)S(1)}, s32[1024,1]{0,1:T(1,128)S(1)}) fusion(s32[]{:T(128)} %bitcast.73, s32[]{:T(128)} %bitcast.74, s32[]{:T(128)} %bitcast.75, s32[]{:T(128)} %bitcast.76, s32[]{:T(128)} %bitcast.77, s32[]{:T(128)} %bitcast.79, s32[]{:T(128)} %bitcast.78, s32[1024,1]{0,1:T(1,128)S(1)} %bitcast.141, ...), kind=kLoop, calls=%fused_computation.89 | loop fusion | flops 14336 | bytes 16412 | tf_op jit(solution)/shard_map/jit(_take)/gather | solution.py:59
  228.6 0.7 compare_reduce_fusion.56
  229.4 35.7 %compare_select_fusion.8 = s32[1024]{0:T(1024)S(1)} fusion(bf16[1024]{0:T(1024)(128)(2,1)S(1)} %all-reduce, pred[1024]{0:T(1024)(128)(4,1)S(1)} %get-tuple-element.70, pred[1024]{0:T(1024)(128)(4,1)S(1)} %get-tuple-element.69, pred[1024]{0:T(1024)(128)(4,1)S(1)} %get-tuple-element.68, pred[1024]{0:T(1024)(128)(4,1)S(1)} %get-tuple-element.67, ...), kind=kLoop, calls=%fused_computation.97 | loop fusion | flops 79872 | bytes 72968 | tf_op jit(solution)/shard_map/select_n | solution.py:64
  265.3 23.3 %all_gather.11 = bf16[1024,2,128]{2,1,0:T(2,128)(2,1)S(1)} all-gather(bf16[64,2,128]{2,1,0:T(2,128)(2,1)S(1)} %copy-done.6), channel_id=1, replica_groups=mesh['req'=16,'mdl'=8] {'req'}, dimensions={0}, use_global_device_ids=true | all-gather | bytes 557056 | tf_op jit(solution)/shard_map/all_gather | solution.py:54
  288.6 30.0 %scatter_fusion = bf16[128,2,128]{2,1,0:T(2,128)(2,1)S(1)} fusion(bf16[128,2,128]{2,1,0:T(2,128)(2,1)S(1)} %bitcast.134, s32[1024]{0:T(1024)S(1)} %broadcast_select_fusion, bf16[1024,2,128]{2,1,0:T(2,128)(2,1)S(1)} %all_gather.11), kind=kCustom, calls=%fused_computation | custom fusion | bytes 1576960
  318.7 1.3 convert_element_type.49
  320.0 1.1 fusion.7
  (44 shorter events, 1.7 us)
Async XLA Ops:
  7.2 52.4 %copy-start = (bf16[1024,512]{1,0:T(8,128)(2,1)S(1)}, bf16[1024,512]{1,0:T(8,128)(2,1)}, u32[]{:S(2)}) copy-start(bf16[1024,512]{1,0:T(8,128)(2,1)} %param.17) | copy-start | bytes 3145732
  7.2 52.4 %all-gather.2.cloned.1.call-start = ((), (), s32[]{:S(2)}) async-start(), calls=%async_computation.1 | async-start | bytes 2228224 | tf_op jit(solution)/shard_map/all_gather | solution.py:66
  11.9 51.6 %copy-start.8 = (bf16[512]{0:T(512)(128)(2,1)S(1)}, bf16[512]{0:T(512)(128)(2,1)}, u32[]{:S(2)}) copy-start(bf16[512]{0:T(512)(128)(2,1)} %param.18) | copy-start | bytes 3076
  11.9 113.4 %copy-start.4 = (bf16[1024,512]{1,0:T(8,128)(2,1)S(1)}, bf16[1024,512]{1,0:T(8,128)(2,1)}, u32[]{:S(2)}) copy-start(bf16[1024,512]{1,0:T(8,128)(2,1)} %param.16) | copy-start | bytes 3145732
  11.9 113.4 %all-reduce.3.cloned.1.call-start = ((), (), s32[]{:S(2)}) async-start(), calls=%async_computation.2 | async-start | bytes 2097152 | tf_op jit(solution)/shard_map/psum | solution.py:71
  63.4 255.2 %reduce-scatter.2.cloned.1.call-start = ((), (), s32[]{:S(2)}) async-start(), calls=%async_computation.3 | async-start | bytes 16154624 | tf_op jit(solution)/shard_map/reduce_scatter | solution.py:80
  125.3 42.3 %copy-start.5 = (bf16[1024,512]{1,0:T(8,128)(2,1)S(1)}, bf16[1024,512]{1,0:T(8,128)(2,1)}, u32[]{:S(2)}) copy-start(bf16[1024,512]{1,0:T(8,128)(2,1)} %all-reduce.3.cloned.1.call-done) | copy-start | bytes 3145732
  182.4 0.7 copy-start.11
  182.4 38.9 %copy-start.3 = (s32[64]{0:T(128)S(1)}, s32[64]{0:T(128)}, u32[]{:S(2)}) copy-start(s32[64]{0:T(128)} %param.14) | copy-start | bytes 772
  182.4 41.8 %copy-start.7 = (s32[8,128]{1,0:T(8,128)S(1)}, s32[8,128]{1,0:T(8,128)}, u32[]{:S(2)}) copy-start(s32[8,128]{1,0:T(8,128)} %constant.119.clone.1) | copy-start | bytes 12292
  182.4 82.7 %copy-start.10 = (s32[2]{0:T(128)S(1)}, s32[2]{0:T(128)}, u32[]{:S(2)}) copy-start(s32[2]{0:T(128)} %constant.129) | copy-start | bytes 28
  182.4 82.8 %copy-start.9 = (s32[2]{0:T(128)S(1)}, s32[2]{0:T(128)}, u32[]{:S(2)}) copy-start(s32[2]{0:T(128)} %constant.132) | copy-start | bytes 28
  182.4 82.9 %copy-start.6 = (bf16[64,2,128]{2,1,0:T(2,128)(2,1)S(1)}, bf16[64,2,128]{2,1,0:T(2,128)(2,1)}, u32[]{:S(2)}) copy-start(bf16[64,2,128]{2,1,0:T(2,128)(2,1)} %param.13) | copy-start | bytes 98308
  182.4 106.1 %copy-start.2 = (bf16[8,16,2,128]{3,2,1,0:T(2,128)(2,1)S(1)}, bf16[8,16,2,128]{3,2,1,0:T(2,128)(2,1)}, u32[]{:S(2)}) copy-start(bf16[8,16,2,128]{3,2,1,0:T(2,128)(2,1)} %param.15) | copy-start | bytes 196612
  318.6 2.5 copy-start.1
Sparse Core Ops, SparseCore 0:
  12.0 47.5 all-gather.1
  63.6 61.7 all-reduce.2
  182.6 99.0 reduce-scatter.1
where the time goes:
time: 329 us; the launch traced here: 328 us
  waiting for transfers between devices  110 us (33%)
  blocking collectives  101 us (31%)
  other arithmetic  46.8 us (14%)
  local copies, waits for them, and re-layouts  36 us (11%)
  matrix products  20 us (6%)
  between operations  14.6 us (4%)
    psum x1, waiting for transfers between devices, on_device(): lax.psum(partial_value.astype(jnp.bfloat16), 'mdl').astype(jnp.float32)  61.8 us
    all_gather x1, waiting for transfers between devices, on_device(): lax.all_gather(attended, 'req', axis=0, tiled=True)  47.6 us
    psum x1, blocking collectives, on_device(): totals = lax.psum(squares, 'req')  40.6 us
    unnamed x1, blocking collectives  36.8 us
    select_n x2, other arithmetic, on_device(): cache_new = paged_cache.at[target, offsets].set(every_pair, mode='drop')  35.7 us
    unnamed x29, local copies, waits for them, and re-layouts  32.2 us
    all_gather x1, blocking collectives, on_device(): lax.all_gather(keys_values, 'req', axis=0, tiled=True)  23.3 us
    dot_general x1, matrix products, on_device(): jnp.dot(normed, flat_weight, preferred_element_type=jnp.float32)  14.8 us
  transfers between devices with their start and end apart: 3, of which 2 were waited for; matrix products, arithmetic and copies ran while one was open for 23% of the time, Pallas kernels for 0%

commit v1 on v0

v1 whole, which is shorter than its diff:
```python
import functools

import jax
import jax.numpy as jnp
from jax import lax
from jax.experimental import pallas as pl
from jax.experimental.pallas import tpu as pltpu
from jax.sharding import PartitionSpec as P

D = 8192
HD = 128
QPK = 8
PAGE = 16
EPSILON = 1e-06
MESH = pl.DeviceIdType.MESH
F32 = jnp.float32
BF16 = jnp.bfloat16
DEAD = 512.0
NT = (((1,), (1,)), ((), ()))


def position():
    req, mdl = lax.axis_index("req"), lax.axis_index("mdl")
    return req // 4, req % 4, mdl // 2, mdl % 2


def dev(y, z, x, c):
    return (y * 4 + z, x * 2 + c)


def ring(v, step):
    return lax.rem(v + step + 4, 4)


def barrier(peers):
    sem = pltpu.get_barrier_semaphore()
    for peer in peers:
        pl.semaphore_signal(sem, inc=1, device_id=peer, device_id_type=MESH)
    pl.semaphore_wait(sem, len(peers))


def copy_to(src, dst, ssem, rsem, peer):
    return pltpu.make_async_remote_copy(
        src_ref=src, dst_ref=dst, send_sem=ssem, recv_sem=rsem, device_id=peer, device_id_type=MESH
    )


def front_kernel(
    q_ref, k_ref, v_ref, segc_ref, segr_ref, pages_ref, cache_ref, res_ref, ow_ref, gain_ref,
    ng_ref, cout_ref,
    ag, acc_own, p2s, p2r, s2s, s2r, chunk_own, n2,
    ag_ss, ag_rs, p_ss, p_rs, x_ss, x_rs, n_ss, n_rs,
):
    y, z, x, c = position()
    me = (y, z, x, c)
    zp, zm = dev(y, ring(z, 1), x, c), dev(y, ring(z, -1), x, c)
    yp, ym = dev(ring(y, 1), z, x, c), dev(ring(y, -1), z, x, c)
    xp, xm = dev(y, z, ring(x, 1), c), dev(y, z, ring(x, -1), c)
    partner = dev(y, z, x, 1 - c)
    barrier((zp, zm, yp, ym, xp, xm, partner))
    started = []

    def go(copy):
        copy.start()
        started.append(copy)
        return copy

    segc, segr = segc_ref[...], segr_ref[...]
    row = lax.broadcasted_iota(jnp.int32, (64, 64), 0)
    col = lax.broadcasted_iota(jnp.int32, (64, 64), 1)
    allowed = ((segc == segr) & (segc >= 0) & (col < row)) | (col == row)
    live = segc >= 0
    keys, values = k_ref[...], v_ref[...]
    for h in range(QPK):
        s = lax.dot_general(q_ref[:, h * HD : (h + 1) * HD], keys, NT, preferred_element_type=F32)
        s = jnp.where(allowed, s * HD ** (-0.5), -jnp.inf)
        w = jnp.exp(s - jnp.max(s, axis=-1, keepdims=True))
        probs = (w / jnp.sum(w, axis=-1, keepdims=True)).astype(BF16)
        mixed = jnp.dot(probs, values, preferred_element_type=F32)
        half, at = h // 4, (h % 4) * HD
        ag[half, y, z, :, at : at + HD] = jnp.where(live, mixed, 0.0).astype(BF16)
    ag[0, y, z, :, 512:640] = jnp.where(live, keys.astype(F32), DEAD).astype(BF16)
    ag[1, y, z, :, 512:640] = jnp.where(live, values.astype(F32), DEAD).astype(BF16)

    first = ((zp, zm), (yp, ym))
    second = ((yp, ym), (zp, zm))

    def spot(half, f, s):
        return (s, f) if half == 0 else (f, s)

    fc, sc = (z, y), (y, z)

    def block(half, f, s, lo=0, n=64):
        a, b = spot(half, f, s)
        return ag.at[half, a, b, pl.ds(lo, n)]

    def ag_copy(half, j, k, ref, peer):
        return copy_to(ref, ref, ag_ss.at[half, j, k], ag_rs.at[half, j, k], peer)

    one = [[None] * 4 for _ in range(2)]
    two = [[[None] * 4 for _ in range(4)] for _ in range(2)]
    offs = (0, -1, 1, 2)

    def start_one(half):
        ref = block(half, fc[half], sc[half])
        for k in range(2):
            one[half][k] = go(ag_copy(half, 4, k, ref, first[half][k]))

    def forward_one(half, k):
        one[half][k].wait_recv()
        ref = block(half, ring(fc[half], -1 if k == 0 else 1), sc[half], 32 * k, 32)
        one[half][2 + k] = go(ag_copy(half, 4, 2 + k, ref, first[half][k]))

    def start_two(half, j):
        ref = block(half, ring(fc[half], offs[j]), sc[half])
        for k in range(2):
            two[half][j][k] = go(ag_copy(half, j, k, ref, second[half][k]))

    def forward_two(half, j):
        for k in range(2):
            two[half][j][k].wait_recv()
            ref = block(half, ring(fc[half], offs[j]), ring(sc[half], -1 if k == 0 else 1), 32 * k, 32)
            two[half][j][2 + k] = go(ag_copy(half, j, 2 + k, ref, second[half][k]))

    def finish_one(half):
        for k in (2, 3):
            one[half][k].wait_recv()

    def finish_two(half, j):
        for k in (2, 3):
            two[half][j][k].wait_recv()

    p_copy = [None] * 4

    def project(g):
        ya = ring(y, offs[g])
        acc = jnp.dot(ag[0, ya, :, :, :512].reshape(256, 512), ow_ref[:512], preferred_element_type=F32)
        acc += jnp.dot(ag[1, ya, :, :, :512].reshape(256, 512), ow_ref[512:], preferred_element_type=F32)
        low, high = acc[:, :256], acc[:, 256:]
        acc_own[g] = jnp.where(c == 0, low, high)
        p2s[g] = jnp.where(c == 0, high, low).astype(BF16)
        p_copy[g] = go(copy_to(p2s.at[g], p2r.at[g], p_ss.at[g], p_rs.at[g], partner))

    for half in range(2):
        start_one(half)
    for half in range(2):
        start_two(half, 0)
    for half in range(2):
        for k in range(2):
            forward_one(half, k)
            start_two(half, 1 + k)
    for half in range(2):
        forward_two(half, 0)
    for half in range(2):
        finish_one(half)
        start_two(half, 3)
    finish_two(1, 0)
    project(0)
    for half in range(2):
        for j in (1, 2):
            forward_two(half, j)
    for half in range(2):
        forward_two(half, 3)
    finish_two(1, 1)
    project(1)
    finish_two(1, 2)
    project(2)
    finish_two(1, 3)
    for j in range(4):
        finish_two(0, j)
    project(3)

    x_copy = [[None] * 10 for _ in range(4)]
    n_copy = [None] * 4
    top, bot = slice(0, 32), slice(32, 64)

    def xmsg(g, i, k, rows, peer):
        return go(copy_to(s2s.at[g, k, rows], s2r.at[g, k, rows], x_ss.at[g, i], x_rs.at[g, i], peer))

    ds_top, ds_bot = pl.ds(0, 32), pl.ds(32, 32)
    for g in range(4):
        p_copy[g].wait_recv()

        def part(xx):
            rows = pl.ds(pl.multiple_of(xx * 64, 64), 64)
            return acc_own[g, rows, :] + p2r[g, rows, :].astype(F32)

        s2s[g, 0] = part(ring(x, 2)).astype(BF16)
        x_copy[g][0] = xmsg(g, 0, 0, ds_top, xp)
        x_copy[g][1] = xmsg(g, 1, 0, ds_bot, xm)
        s2s[g, 1] = part(ring(x, 1)).astype(BF16)
        x_copy[g][2] = xmsg(g, 2, 1, ds_bot, xp)
        s2s[g, 2] = part(ring(x, -1)).astype(BF16)
        x_copy[g][3] = xmsg(g, 3, 2, ds_top, xm)
        chunk_own[g] = part(x)
    for g in range(4):
        x_copy[g][0].wait_recv()
        s2s[g, 1, top] = (s2s[g, 1, top].astype(F32) + s2r[g, 0, top].astype(F32)).astype(BF16)
        x_copy[g][4] = xmsg(g, 4, 1, ds_top, xp)
        x_copy[g][1].wait_recv()
        s2s[g, 2, bot] = (s2s[g, 2, bot].astype(F32) + s2r[g, 0, bot].astype(F32)).astype(BF16)
        x_copy[g][5] = xmsg(g, 5, 2, ds_bot, xm)

    def nmsg(g, i, ref, peer):
        return go(copy_to(ref, ref, x_ss.at[g, i], x_rs.at[g, i], peer))

    gain = jnp.where(c == 0, gain_ref[:, :256], gain_ref[:, 256:])
    for g in range(4):
        ya = ring(y, offs[g])
        for i in (2, 3, 4, 5):
            x_copy[g][i].wait_recv()
        total = chunk_own[g] + s2r[g, 1].astype(F32) + s2r[g, 2].astype(F32)
        res = res_ref[ya, x].astype(F32)
        stream = total + jnp.where(c == 0, res[:, :256], res[:, 256:])
        n2[ya, c, x] = (stream * gain).astype(BF16)
        ref = n2.at[ya, c, x]
        x_copy[g][6] = nmsg(g, 6, ref, xp)
        x_copy[g][7] = nmsg(g, 7, ref, xm)
    for g in range(4):
        ya = ring(y, offs[g])
        x_copy[g][6].wait_recv()
        x_copy[g][8] = nmsg(g, 8, n2.at[ya, c, ring(x, -1), ds_top], xp)
        x_copy[g][7].wait_recv()
        x_copy[g][9] = nmsg(g, 9, n2.at[ya, c, ring(x, 1), ds_bot], xm)
    for g in range(4):
        ya = ring(y, offs[g])
        x_copy[g][8].wait_recv()
        x_copy[g][9].wait_recv()
        ref = n2.at[ya, c]
        n_copy[g] = go(copy_to(ref, ref, n_ss.at[g], n_rs.at[g], partner))

    req = lax.axis_index("req")
    base = req * 8
    slot = lax.broadcasted_iota(jnp.int32, (128, 1024), 0)
    tok = lax.broadcasted_iota(jnp.int32, (128, 1024), 1)
    hit = (pages_ref[...] == base + slot // PAGE) & (slot % PAGE == tok % PAGE)
    pick = jnp.where(hit, 1.0, 0.0)
    has = jnp.sum(pick, axis=1, keepdims=True) > 0.5
    pick = pick.astype(BF16)
    for half in range(2):
        new = jnp.dot(pick, ag[half, :, :, :, 512:640].reshape(1024, 128), preferred_element_type=F32)
        old = cache_ref[:, half * 128 : half * 128 + 128]
        cout_ref[:, half * 128 : half * 128 + 128] = jnp.where(
            has & (new < 0.5 * DEAD), new, old.astype(F32)
        ).astype(BF16)

    for g in range(4):
        ya = ring(y, offs[g])
        n_copy[g].wait_recv()
        for h in range(2):
            ng_ref[ya, :, :, h * 256 : h * 256 + 256] = n2[ya, h]
    for copy in started:
        copy.wait_send()


def front(q, k, v, segc, segr, pages, cache, res, ow, gain):
    vm = pl.BlockSpec(memory_space=pltpu.VMEM)
    dma = pltpu.SemaphoreType.DMA
    return pl.pallas_call(
        front_kernel,
        out_shape=(
            jax.ShapeDtypeStruct((4, 4, 64, 512), BF16),
            jax.ShapeDtypeStruct((128, 256), BF16),
        ),
        in_specs=[vm] * 10,
        out_specs=(vm, vm),
        scratch_shapes=[
            pltpu.VMEM((2, 4, 4, 64, 640), BF16),
            pltpu.VMEM((4, 256, 256), F32),
            pltpu.VMEM((4, 256, 256), BF16),
            pltpu.VMEM((4, 256, 256), BF16),
            pltpu.VMEM((4, 3, 64, 256), BF16),
            pltpu.VMEM((4, 3, 64, 256), BF16),
            pltpu.VMEM((4, 64, 256), F32),
            pltpu.VMEM((4, 2, 4, 64, 256), BF16),
            dma((2, 5, 4)), dma((2, 5, 4)),
            dma((4,)), dma((4,)),
            dma((4, 10)), dma((4, 10)),
            dma((4,)), dma((4,)),
        ],
        compiler_params=pltpu.CompilerParams(collective_id=0, has_side_effects=True, vmem_limit_bytes=60 << 20),
        name="front",
    )(q, k, v, segc, segr, pages, cache, res, ow, gain)


WIDE = 3712
COLS = 3696
PIECES = ((2688, 1024), (0, 896), (896, 896), (1792, 896))


def back_kernel(
    ng_ref, ginv_ref, w_ref, out_ref,
    w, ss, own1, own2, rscale, s1, r1, s2, r2,
    w_sem, ss1, rs1, ss2, rs2,
):
    y, z, x, c = position()
    zp, zm = dev(y, ring(z, 1), x, c), dev(y, ring(z, -1), x, c)
    yp, ym = dev(ring(y, 1), z, x, c), dev(ring(y, -1), z, x, c)
    loads = []
    for p, (lo, n) in enumerate(PIECES):
        for g in range(2):
            m = min(n, COLS - lo)
            loads.append(
                pltpu.make_async_copy(w_ref.at[g, pl.ds(lo, m)], w.at[g, pl.ds(lo, m)], w_sem.at[p, g])
            )
            loads[-1].start()
    barrier((zp, zm, yp, ym))
    started = []

    def go(copy):
        copy.start()
        started.append(copy)
        return copy

    first = ((zp, zm), (yp, ym))
    second = ((yp, ym), (zp, zm))
    fc, sc = (z, y), (y, z)
    r = lax.axis_index("req")
    ginv = ginv_ref[...]
    for a in range(4):
        v = ng_ref[a].reshape(256, 512).astype(F32) * ginv
        ss[a] = jnp.broadcast_to(jnp.sum(v * v, axis=1, keepdims=True), (256, 128)).reshape(4, 64, 128)

    def rows_of(ref, g, d, n):
        v = ref[:, pl.ds(d, 1)] if g == 0 else ref[pl.ds(d, 1)]
        return v.reshape(256, n)

    def partial(g, d, p):
        lo, n = PIECES[p]
        out = lax.dot_general(rows_of(ng_ref, g, d, 512), w[g, lo : lo + n], NT, preferred_element_type=F32)
        if lo + n > COLS:
            tot = rows_of(ss, g, d, 128)
            high = tot.astype(BF16).astype(F32)
            mine = high if g == 0 else tot - high
            lane = lax.broadcasted_iota(jnp.int32, (256, 128), 1)
            tail = out[:, n - 128 :]
            tail = jnp.where(lane < 112, tail, jnp.where(lane == 112 + r, mine, 0.0))
            out = jnp.concatenate([out[:, : n - 128], tail], axis=1)
        return out.reshape(4, 64, n)

    one = [[[None] * 6 for _ in range(2)] for _ in range(4)]
    two = [[[None] * 6 for _ in range(2)] for _ in range(4)]

    def send1(p, g, i, k, t, peer):
        lo, n = PIECES[p]
        at = (g, k, pl.ds(t, 2), slice(None), pl.ds(lo, n))
        one[p][g][i] = go(copy_to(s1.at[at], r1.at[at], ss1.at[p, g, i], rs1.at[p, g, i], peer))

    def send2(p, g, i, k, t, peer):
        lo, n = PIECES[p]
        at = (g, k, pl.ds(t, 32), pl.ds(lo, n))
        two[p][g][i] = go(copy_to(s2.at[at], r2.at[at], ss2.at[p, g, i], rs2.at[p, g, i], peer))

    def stage_x(p):
        lo, n = PIECES[p]
        hi = lo + n
        for g in range(2):
            loads[2 * p + g].wait()
            s1[g, 0, :, :, lo:hi] = partial(g, ring(fc[g], 2), p).astype(BF16)
            send1(p, g, 0, 0, 0, first[g][0])
            send1(p, g, 1, 0, 2, first[g][1])
        for g in range(2):
            s1[g, 1, :, :, lo:hi] = partial(g, ring(fc[g], 1), p).astype(BF16)
            send1(p, g, 2, 1, 2, first[g][0])
            s1[g, 2, :, :, lo:hi] = partial(g, ring(fc[g], -1), p).astype(BF16)
            send1(p, g, 3, 2, 0, first[g][1])

    def stage_y(p):
        lo, n = PIECES[p]
        hi = lo + n
        for g in range(2):
            for k in range(2):
                t = 2 * k
                one[p][g][k].wait_recv()
                v = s1[g, 1 + k, t : t + 2, :, lo:hi].astype(F32) + r1[g, 0, t : t + 2, :, lo:hi].astype(F32)
                s1[g, 1 + k, t : t + 2, :, lo:hi] = v.astype(BF16)
                send1(p, g, 4 + k, 1 + k, t, first[g][k])

    def stage_z(p):
        lo, n = PIECES[p]
        hi = lo + n
        for g in range(2):
            own1[g, :, :, :n] = partial(g, fc[g], p)
        for g in range(2):
            for i in (2, 3, 4, 5):
                one[p][g][i].wait_recv()

            def summed(t):
                at = (pl.ds(t, 1), slice(None))
                return (
                    own1[g, pl.ds(t, 1), :, :n]
                    + r1[g, 1, pl.ds(t, 1), :, lo:hi].astype(F32)
                    + r1[g, 2, pl.ds(t, 1), :, lo:hi].astype(F32)
                ).reshape(64, n)

            s2[g, 0, :, lo:hi] = summed(ring(sc[g], 2)).astype(BF16)
            send2(p, g, 0, 0, 0, second[g][0])
            send2(p, g, 1, 0, 32, second[g][1])
            s2[g, 1, :, lo:hi] = summed(ring(sc[g], 1)).astype(BF16)
            send2(p, g, 2, 1, 32, second[g][0])
            s2[g, 2, :, lo:hi] = summed(ring(sc[g], -1)).astype(BF16)
            send2(p, g, 3, 2, 0, second[g][1])
            own2[g, :, lo:hi] = summed(sc[g])

    def stage_u(p):
        lo, n = PIECES[p]
        hi = lo + n
        for g in range(2):
            for k in range(2):
                t = 32 * k
                two[p][g][k].wait_recv()
                v = s2[g, 1 + k, t : t + 32, lo:hi].astype(F32) + r2[g, 0, t : t + 32, lo:hi].astype(F32)
                s2[g, 1 + k, t : t + 32, lo:hi] = v.astype(BF16)
                send2(p, g, 4 + k, 1 + k, t, second[g][k])

    def stage_v(p):
        lo, n = PIECES[p]
        hi = lo + n
        val = []
        for g in range(2):
            for i in (2, 3, 4, 5):
                two[p][g][i].wait_recv()
            val.append(own2[g, :, lo:hi] + r2[g, 1, :, lo:hi].astype(F32) + r2[g, 2, :, lo:hi].astype(F32))
        if hi > COLS:
            lane = lax.broadcasted_iota(jnp.int32, (64, 128), 1)
            tail = val[0][:, n - 128 :] + val[1][:, n - 128 :]
            tot = jnp.sum(jnp.where(lane >= 112, tail, 0.0), axis=1, keepdims=True)
            rscale[...] = jnp.broadcast_to(lax.rsqrt(tot / D + EPSILON), (64, 128))
        scale = rscale[:, :1]
        gate, up = val[0] * scale, val[1] * scale
        hidden = (gate / (1.0 + jnp.exp(-gate)) * up).astype(BF16)
        m = min(n, COLS - lo)
        out_ref[:, lo : lo + m] = hidden[:, :m]

    for stage, p in (
        (stage_x, 0), (stage_x, 1), (stage_y, 0), (stage_x, 2), (stage_y, 1), (stage_z, 0),
        (stage_x, 3), (stage_y, 2), (stage_z, 1), (stage_u, 0), (stage_y, 3), (stage_z, 2),
        (stage_u, 1), (stage_v, 0), (stage_z, 3), (stage_u, 2), (stage_v, 1), (stage_u, 3),
        (stage_v, 2), (stage_v, 3),
    ):
        stage(p)
    for copy in started:
        copy.wait_send()


def back(ng, ginv, wt):
    vm = pl.BlockSpec(memory_space=pltpu.VMEM)
    dma = pltpu.SemaphoreType.DMA
    return pl.pallas_call(
        back_kernel,
        out_shape=jax.ShapeDtypeStruct((64, COLS), BF16),
        in_specs=[vm, vm, pl.BlockSpec(memory_space=pl.ANY)],
        out_specs=vm,
        scratch_shapes=[
            pltpu.VMEM((2, WIDE, 512), BF16),
            pltpu.VMEM((4, 4, 64, 128), F32),
            pltpu.VMEM((2, 4, 64, 1024), F32),
            pltpu.VMEM((2, 64, WIDE), F32),
            pltpu.VMEM((64, 128), F32),
            pltpu.VMEM((2, 3, 4, 64, WIDE), BF16),
            pltpu.VMEM((2, 3, 4, 64, WIDE), BF16),
            pltpu.VMEM((2, 3, 64, WIDE), BF16),
            pltpu.VMEM((2, 3, 64, WIDE), BF16),
            dma((4, 2)),
            dma((4, 2, 6)), dma((4, 2, 6)),
            dma((4, 2, 6)), dma((4, 2, 6)),
        ],
        compiler_params=pltpu.CompilerParams(collective_id=1, has_side_effects=True, vmem_limit_bytes=67043328),
        name="back",
    )(ng, ginv, wt)


def on_device(
    segments, queries, keys_values, page_table, paged_cache, residual, out_weight, norm_gain, gate_up_weight
):
    keys, values = keys_values[:, 0], keys_values[:, 1]
    pages = jnp.broadcast_to(page_table[:, None], (64, PAGE)).reshape(1, 1024)
    gain = norm_gain.astype(F32)[None, :]
    ng, cache = front(
        queries, keys, values, segments[:, None], segments[None, :], pages,
        paged_cache.reshape(128, 256), residual.reshape(4, 4, 64, 512), out_weight, gain,
    )
    wt = gate_up_weight.transpose(1, 2, 0)
    hidden = back(ng, 1.0 / gain, wt)
    return hidden, cache.reshape(8, 16, 2, 128)


def solution(mesh):
    placed = (
        P("req"),
        P("req", "mdl"),
        P("req", None, "mdl"),
        P(),
        P("req", None, None, "mdl"),
        P(None, "req"),
        P("mdl", "req"),
        P("req"),
        P("req", None, "mdl"),
    )
    return jax.shard_map(
        on_device,
        mesh=mesh,
        in_specs=placed,
        out_specs=(P("req", "mdl"), P("req", None, None, "mdl")),
        check_vma=False,
    )
```

time: 329 us -> 148 us (0.45)
  Pallas kernels: 0 us -> 135 us
  waiting for transfers between devices: 110 us -> 0 us
  blocking collectives: 101 us -> 0 us
  other arithmetic: 46.8 us -> 2.52 us
  local copies, waits for them, and re-layouts: 36 us -> 9.08 us
  matrix products: 20 us -> 0 us
  between operations: 14.6 us -> 0.65 us
    pallas_call x0 -> x2, Pallas kernels: none -> 135 us  [the longest x1 87.6 us: back(): pl.pallas_call(back_kernel, out_shape=jax.ShapeDtypeStruct((64, COLS), BF...]
    psum x1 -> x0, waiting for transfers between devices: 61.8 us -> none  [on_device(): lax.psum(partial_value.astype(jnp.bfloat16), 'mdl').astype(jnp.float32)]
    all_gather x1 -> x0, waiting for transfers between devices: 47.6 us -> none  [on_device(): lax.all_gather(attended, 'req', axis=0, tiled=True)]
    psum x1 -> x0, blocking collectives: 40.6 us -> none  [on_device(): totals = lax.psum(squares, 'req')]
    unnamed x1 -> x0, blocking collectives: 36.8 us -> none
    select_n x2 -> x0, other arithmetic: 35.7 us -> none  [on_device(): cache_new = paged_cache.at[target, offsets].set(every_pair, mode='drop')]
    unnamed x29 -> x2, local copies, waits for them, and re-layouts: 32.2 us -> 3.31 us
    all_gather x1 -> x0, blocking collectives: 23.3 us -> none  [on_device(): lax.all_gather(keys_values, 'req', axis=0, tiled=True)]
  transfers between devices with their start and end apart: 3 -> 0, of which waited for: 2 -> 0; matrix products, arithmetic and copies ran while one was open for 23% -> 0% of each run, Pallas kernels for 0% -> 0%
where the time goes in v1:
time: 148 us; the launch traced here: 147 us
  Pallas kernels  135 us (91%)
  local copies, waits for them, and re-layouts  9.08 us (6%)
  other arithmetic  2.52 us (2%)
    pallas_call x1, Pallas kernels, back(): pl.pallas_call(back_kernel, out_shape=jax.ShapeDtypeStruct((64, COLS), BF...  87.6 us
    pallas_call x1, Pallas kernels, front(): pl.pallas_call(front_kernel, out_shape=(jax.ShapeDtypeStruct((4, 4, 64, 5...  47.2 us
    unnamed x2, local copies, waits for them, and re-layouts  3.31 us

profile of v1, /device:TPU:0, one launch (start us, length us, event | category | flops | bytes accessed | tf_op | source)
XLA Modules:
  0.0 147.1 jit_solution(14578509057026247462)
XLA Ops:
  0.6 1.3 broadcast_divide_fusion
  1.9 1.3 convert_element_type.3
  3.2 0.7 broadcast_in_dim.17
  3.9 0.7 reshape.18.pages_ref
  4.6 1.4 copy.16.segc_ref
  5.9 1.5 %copy.23 = bf16[16,8,2,128]{3,1,2,0:T(8,128)(2,1)} copy(bf16[16,8,2,128]{3,2,1,0:T(2,128)(2,1)} %bitcast.18) | data formatting | bytes 131072
  7.4 0.9 fusion
  8.3 0.6 copy_bitcast_fusion.1
  8.9 47.2 %front.1 = (bf16[4,4,64,512]{3,2,1,0:T(8,128)(2,1)}, bf16[128,256]{1,0:T(8,128)(2,1)}) custom-call(bf16[64,1024]{1,0:T(8,128)(2,1)} %q_ref.1, bf16[64,128]{1,0:T(8,128)(2,1)} %get-tuple-element.9.k_ref, bf16[64,128]{1,0:T(8,128)(2,1)} %get-tuple-element.8.v_ref, s32[64,1]{1,0:T(8,128)} %copy.16.segc_ref, s32[1,64]{1,0:T(1,128)} %bitcast.22, ...), custom_call_target="tpu_custom_call" | custom-call | tf_op jit(solution)/shard_map/front/pallas_call | solution.py:259
  56.1 87.6 %back.1 = bf16[64,3696]{1,0:T(8,128)(2,1)} custom-call(bf16[4,4,64,512]{3,2,1,0:T(8,128)(2,1)} %get-tuple-element.4.ng_ref, f32[1,512]{1,0:T(1,128)} %bitcast.19, bf16[2,3696,512]{2,1,0:T(8,128)(2,1)} %bitcast.15), custom_call_target="tpu_custom_call" | custom-call | tf_op jit(solution)/shard_map/back/pallas_call | solution.py:449
  143.8 1.5 %reshape.21 = bf16[8,16,2,128]{3,2,1,0:T(2,128)(2,1)} reshape(bf16[128,256]{1,0:T(8,128)(2,1)} %get-tuple-element.5) | data formatting | bytes 131072 | tf_op jit(solution)/shard_map/reshape | solution.py:485
  145.3 1.8 %copy.25 = bf16[64,3696]{1,0:T(8,128)(2,1)} copy(bf16[64,3696]{1,0:T(8,128)(2,1)} %back.1) | data formatting | bytes 946176

commit v2 on v1

v2 whole, which is shorter than its diff:
```python
import jax
import jax.numpy as jnp
from jax import lax
from jax.experimental import pallas as pl
from jax.experimental.pallas import tpu as pltpu
from jax.sharding import PartitionSpec as P

D = 8192
HD = 128
QPK = 8
PAGE = 16
EPSILON = 1e-06
MESH = pl.DeviceIdType.MESH
F32 = jnp.float32
BF16 = jnp.bfloat16
DEAD = 512.0
NT = (((1,), (1,)), ((), ()))


def position():
    req, mdl = lax.axis_index("req"), lax.axis_index("mdl")
    return req // 4, req % 4, mdl // 2, mdl % 2


def dev(y, z, x, c):
    return (y * 4 + z, x * 2 + c)


def ring(v, step):
    return lax.rem(v + step + 4, 4)


def barrier(peers):
    sem = pltpu.get_barrier_semaphore()
    for peer in peers:
        pl.semaphore_signal(sem, inc=1, device_id=peer, device_id_type=MESH)
    pl.semaphore_wait(sem, len(peers))


def copy_to(src, dst, ssem, rsem, peer):
    return pltpu.make_async_remote_copy(
        src_ref=src, dst_ref=dst, send_sem=ssem, recv_sem=rsem, device_id=peer, device_id_type=MESH
    )


WIDE = 3712
COLS = 3696
PIECES = ((2688, 1024), (0, 896), (896, 896), (1792, 896))


def layer_kernel(
    seg_ref, pages_ref, gain_ref, q_ref, kv_ref, cache_ref, res_hbm, ow_hbm, w_ref,
    out_ref, cout_ref,
    res_ref, ow_ref, ag, kvb, acc_own, p2s, p2r, s2s, s2r, chunk_own, n2, ng_ref,
    w, ss, own1, own2, rscale, s1, r1, s2, r2,
    in_sem, w_sem, ag_ss, ag_rs, kv_ss, kv_rs, p_ss, p_rs, x_ss, x_rs, n_ss, n_rs,
    ss1, rs1, ss2, rs2,
):
    y, z, x, c = position()
    zp, zm = dev(y, ring(z, 1), x, c), dev(y, ring(z, -1), x, c)
    yp, ym = dev(ring(y, 1), z, x, c), dev(ring(y, -1), z, x, c)
    xp, xm = dev(y, z, ring(x, 1), c), dev(y, z, ring(x, -1), c)
    partner = dev(y, z, x, 1 - c)
    ow_load = pltpu.make_async_copy(ow_hbm, ow_ref, in_sem.at[0])
    res_load = pltpu.make_async_copy(res_hbm, res_ref, in_sem.at[1])
    ow_load.start()
    res_load.start()
    loads = []
    for p, (lo, n) in enumerate(PIECES):
        for g in range(2):
            m = min(n, COLS - lo)
            loads.append(
                pltpu.make_async_copy(w_ref.at[g, pl.ds(lo, m)], w.at[g, pl.ds(lo, m)], w_sem.at[p, g])
            )
            loads[-1].start()
    started = []

    def go(copy):
        copy.start()
        started.append(copy)
        return copy

    seg = jnp.broadcast_to(seg_ref[...].astype(F32), (128, 64))
    wide_row = lax.broadcasted_iota(jnp.int32, (128, 64), 0)
    wide_col = lax.broadcasted_iota(jnp.int32, (128, 64), 1)
    seg_kv = jnp.sum(jnp.where(wide_col == wide_row // 2, seg, 0.0), axis=1, keepdims=True)
    segc = jnp.sum(jnp.where(wide_col == wide_row, seg, 0.0)[:64], axis=1, keepdims=True)
    row = lax.broadcasted_iota(jnp.int32, (64, 128), 0)
    col = lax.broadcasted_iota(jnp.int32, (64, 128), 1)
    segr = jnp.sum(jnp.where(col // 2 == row, segc, 0.0), axis=0, keepdims=True)
    allowed = ((segc == segr) & (segc >= 0) & (col // 2 < row)) | (col // 2 == row)
    allowed = allowed & (col % 2 == 0)
    live = segc >= 0
    kv = kv_ref[...]
    for h in range(QPK):
        s = lax.dot_general(q_ref[:, h * HD : (h + 1) * HD], kv, NT, preferred_element_type=F32)
        s = jnp.where(allowed, s * HD ** (-0.5), -jnp.inf)
        e = jnp.exp(s - jnp.max(s, axis=-1, keepdims=True))
        probs = pltpu.roll(e / jnp.sum(e, axis=-1, keepdims=True), 1, 1).astype(BF16)
        mixed = jnp.dot(probs, kv, preferred_element_type=F32)
        half, at = h // 4, (h % 4) * HD
        ag[half, y, z, :, at : at + HD] = jnp.where(live, mixed, 0.0).astype(BF16)
    kvb[y, z] = jnp.where(seg_kv >= 0, kv.astype(F32), DEAD).astype(BF16)
    barrier((zp, zm, yp, ym, xp, xm, partner))

    first = ((zp, zm), (yp, ym))
    second = ((yp, ym), (zp, zm))
    fc, sc = (z, y), (y, z)

    def block(half, f, s, lo=0, n=64):
        a, b = (s, f) if half == 0 else (f, s)
        return ag.at[half, a, b, pl.ds(lo, n)]

    def ag_copy(half, j, k, ref, peer):
        return copy_to(ref, ref, ag_ss.at[half, j, k], ag_rs.at[half, j, k], peer)

    one = [[None] * 4 for _ in range(2)]
    two = [[[None] * 4 for _ in range(4)] for _ in range(2)]
    offs = (0, -1, 1, 2)

    def start_one(half):
        ref = block(half, fc[half], sc[half])
        for k in range(2):
            one[half][k] = go(ag_copy(half, 4, k, ref, first[half][k]))

    def forward_one(half, k):
        one[half][k].wait_recv()
        ref = block(half, ring(fc[half], -1 if k == 0 else 1), sc[half], 32 * k, 32)
        one[half][2 + k] = go(ag_copy(half, 4, 2 + k, ref, first[half][k]))

    def start_two(half, j):
        ref = block(half, ring(fc[half], offs[j]), sc[half])
        for k in range(2):
            two[half][j][k] = go(ag_copy(half, j, k, ref, second[half][k]))

    def forward_two(half, j):
        for k in range(2):
            two[half][j][k].wait_recv()
            ref = block(half, ring(fc[half], offs[j]), ring(sc[half], -1 if k == 0 else 1), 32 * k, 32)
            two[half][j][2 + k] = go(ag_copy(half, j, 2 + k, ref, second[half][k]))

    def finish_one(half):
        for k in (2, 3):
            one[half][k].wait_recv()

    def finish_two(half, j):
        for k in (2, 3):
            two[half][j][k].wait_recv()

    kv_copy = [None] * 8

    def kv_msg(i, ref, peer):
        kv_copy[i] = go(copy_to(ref, ref, kv_ss.at[i], kv_rs.at[i], peer))

    def kv_start():
        kv_msg(0, kvb.at[y, z], zp)
        kv_msg(1, kvb.at[y, z], zm)

    def kv_forward():
        kv_copy[0].wait_recv()
        kv_msg(2, kvb.at[y, ring(z, -1), pl.ds(0, 64)], zp)
        kv_copy[1].wait_recv()
        kv_msg(3, kvb.at[y, ring(z, 1), pl.ds(64, 64)], zm)

    def kv_rows():
        kv_copy[2].wait_recv()
        kv_copy[3].wait_recv()
        kv_msg(4, kvb.at[y], yp)
        kv_msg(5, kvb.at[y], ym)

    def kv_rows_forward():
        kv_copy[4].wait_recv()
        kv_msg(6, kvb.at[ring(y, -1), pl.ds(0, 2)], yp)
        kv_copy[5].wait_recv()
        kv_msg(7, kvb.at[ring(y, 1), pl.ds(2, 2)], ym)

    p_copy = [None] * 4
    x_copy = [[None] * 10 for _ in range(4)]
    n_copy = [None] * 4
    top, bot = slice(0, 32), slice(32, 64)
    ds_top, ds_bot = pl.ds(0, 32), pl.ds(32, 32)

    def project(g):
        ya = ring(y, offs[g])
        acc = jnp.dot(ag[0, ya].reshape(256, 512), ow_ref[:512], preferred_element_type=F32)
        acc += jnp.dot(ag[1, ya].reshape(256, 512), ow_ref[512:], preferred_element_type=F32)
        low, high = acc[:, :256], acc[:, 256:]
        acc_own[g] = jnp.where(c == 0, low, high)
        p2s[g] = jnp.where(c == 0, high, low).astype(BF16)
        p_copy[g] = go(copy_to(p2s.at[g], p2r.at[g], p_ss.at[g], p_rs.at[g], partner))

    def xmsg(g, i, k, rows, peer):
        x_copy[g][i] = go(copy_to(s2s.at[g, k, rows], s2r.at[g, k, rows], x_ss.at[g, i], x_rs.at[g, i], peer))

    def reduce_a(g):
        p_copy[g].wait_recv()

        def part(xx):
            rows = pl.ds(pl.multiple_of(xx * 64, 64), 64)
            return acc_own[g, rows, :] + p2r[g, rows, :].astype(F32)

        s2s[g, 0] = part(ring(x, 2)).astype(BF16)
        xmsg(g, 0, 0, ds_top, xp)
        xmsg(g, 1, 0, ds_bot, xm)
        s2s[g, 1] = part(ring(x, 1)).astype(BF16)
        xmsg(g, 2, 1, ds_bot, xp)
        s2s[g, 2] = part(ring(x, -1)).astype(BF16)
        xmsg(g, 3, 2, ds_top, xm)
        chunk_own[g] = part(x)

    def reduce_b(g):
        x_copy[g][0].wait_recv()
        s2s[g, 1, top] = (s2s[g, 1, top].astype(F32) + s2r[g, 0, top].astype(F32)).astype(BF16)
        xmsg(g, 4, 1, ds_top, xp)
        x_copy[g][1].wait_recv()
        s2s[g, 2, bot] = (s2s[g, 2, bot].astype(F32) + s2r[g, 0, bot].astype(F32)).astype(BF16)
        xmsg(g, 5, 2, ds_bot, xm)

    def nmsg(g, i, ref, peer):
        x_copy[g][i] = go(copy_to(ref, ref, x_ss.at[g, i], x_rs.at[g, i], peer))

    gain_row = gain_ref[...].astype(F32)
    gain = jnp.where(c == 0, gain_row[:, :256], gain_row[:, 256:])
    ginv = 1.0 / gain_row

    def reduce_c(g):
        ya = ring(y, offs[g])
        for i in (2, 3, 4, 5):
            x_copy[g][i].wait_recv()
        total = chunk_own[g] + s2r[g, 1].astype(F32) + s2r[g, 2].astype(F32)
        res = res_ref[ya, x].astype(F32)
        stream = total + jnp.where(c == 0, res[:, :256], res[:, 256:])
        n2[ya, c, x] = (stream * gain).astype(BF16)
        nmsg(g, 6, n2.at[ya, c, x], xp)
        nmsg(g, 7, n2.at[ya, c, x], xm)

    def reduce_d(g):
        ya = ring(y, offs[g])
        x_copy[g][6].wait_recv()
        nmsg(g, 8, n2.at[ya, c, ring(x, -1), ds_top], xp)
        x_copy[g][7].wait_recv()
        nmsg(g, 9, n2.at[ya, c, ring(x, 1), ds_bot], xm)

    def reduce_e(g):
        ya = ring(y, offs[g])
        x_copy[g][8].wait_recv()
        x_copy[g][9].wait_recv()
        ref = n2.at[ya, c]
        n_copy[g] = go(copy_to(ref, ref, n_ss.at[g], n_rs.at[g], partner))

    def reduce_f(g):
        ya = ring(y, offs[g])
        n_copy[g].wait_recv()
        squares = 0.0
        for h in range(2):
            at = slice(h * 256, h * 256 + 256)
            v = n2[ya, h]
            ng_ref[ya, :, :, at] = v
            v = v.reshape(256, 256).astype(F32) * ginv[:, at]
            squares += jnp.sum(v * v, axis=1, keepdims=True)
        ss[ya] = jnp.broadcast_to(squares, (256, 128)).reshape(4, 64, 128)

    for half in range(2):
        start_one(half)
    for half in range(2):
        start_two(half, 0)
    for half in range(2):
        for k in range(2):
            forward_one(half, k)
            start_two(half, 1 + k)
    for half in range(2):
        forward_two(half, 0)
    for half in range(2):
        finish_one(half)
        start_two(half, 3)
    kv_start()
    ow_load.wait()
    finish_two(1, 0)
    project(0)
    for j in (1, 2):
        for half in range(2):
            forward_two(half, j)
    reduce_a(0)
    for half in range(2):
        forward_two(half, 3)
    finish_two(1, 1)
    project(1)
    reduce_b(0)
    finish_two(1, 2)
    project(2)
    kv_forward()
    reduce_a(1)
    res_load.wait()
    reduce_c(0)
    reduce_a(2)
    reduce_b(1)
    finish_two(1, 3)
    for j in range(4):
        finish_two(0, j)
    project(3)
    kv_rows()
    reduce_d(0)
    reduce_b(2)
    reduce_c(1)
    reduce_a(3)
    reduce_e(0)
    reduce_d(1)
    reduce_c(2)
    reduce_b(3)
    reduce_e(1)
    reduce_f(0)
    reduce_d(2)
    reduce_c(3)
    reduce_e(2)
    reduce_f(1)
    kv_rows_forward()
    reduce_d(3)
    reduce_f(2)
    reduce_e(3)
    reduce_f(3)

    r = lax.axis_index("req")

    def rows_of(ref, g, d, n):
        v = ref[:, pl.ds(d, 1)] if g == 0 else ref[pl.ds(d, 1)]
        return v.reshape(256, n)

    def partial(g, d, p):
        lo, n = PIECES[p]
        out = lax.dot_general(rows_of(ng_ref, g, d, 512), w[g, lo : lo + n], NT, preferred_element_type=F32)
        if lo + n > COLS:
            tot = rows_of(ss, g, d, 128)
            high = tot.astype(BF16).astype(F32)
            mine = high if g == 0 else tot - high
            lane = lax.broadcasted_iota(jnp.int32, (256, 128), 1)
            tail = out[:, n - 128 :]
            tail = jnp.where(lane < 112, tail, jnp.where(lane == 112 + r, mine, 0.0))
            out = jnp.concatenate([out[:, : n - 128], tail], axis=1)
        return out.reshape(4, 64, n)

    fast = [[[None] * 6 for _ in range(2)] for _ in range(4)]
    slow = [[[None] * 6 for _ in range(2)] for _ in range(4)]

    def send1(p, g, i, k, t, peer):
        lo, n = PIECES[p]
        at = (g, k, pl.ds(t, 2), slice(None), pl.ds(lo, n))
        fast[p][g][i] = go(copy_to(s1.at[at], r1.at[at], ss1.at[p, g, i], rs1.at[p, g, i], peer))

    def send2(p, g, i, k, t, peer):
        lo, n = PIECES[p]
        at = (g, k, pl.ds(t, 32), pl.ds(lo, n))
        slow[p][g][i] = go(copy_to(s2.at[at], r2.at[at], ss2.at[p, g, i], rs2.at[p, g, i], peer))

    def stage_x(p):
        lo, n = PIECES[p]
        hi = lo + n
        for g in range(2):
            loads[2 * p + g].wait()
            s1[g, 0, :, :, lo:hi] = partial(g, ring(fc[g], 2), p).astype(BF16)
            send1(p, g, 0, 0, 0, first[g][0])
            send1(p, g, 1, 0, 2, first[g][1])
        for g in range(2):
            s1[g, 1, :, :, lo:hi] = partial(g, ring(fc[g], 1), p).astype(BF16)
            send1(p, g, 2, 1, 2, first[g][0])
            s1[g, 2, :, :, lo:hi] = partial(g, ring(fc[g], -1), p).astype(BF16)
            send1(p, g, 3, 2, 0, first[g][1])

    def stage_y(p):
        lo, n = PIECES[p]
        hi = lo + n
        for g in range(2):
            for k in range(2):
                t = 2 * k
                fast[p][g][k].wait_recv()
                v = s1[g, 1 + k, t : t + 2, :, lo:hi].astype(F32) + r1[g, 0, t : t + 2, :, lo:hi].astype(F32)
                s1[g, 1 + k, t : t + 2, :, lo:hi] = v.astype(BF16)
                send1(p, g, 4 + k, 1 + k, t, first[g][k])

    def stage_z(p):
        lo, n = PIECES[p]
        hi = lo + n
        for g in range(2):
            own1[g, :, :, :n] = partial(g, fc[g], p)
        for g in range(2):
            for i in (2, 3, 4, 5):
                fast[p][g][i].wait_recv()

            def summed(t):
                at = (pl.ds(t, 1), slice(None))
                return (
                    own1[g, pl.ds(t, 1), :, :n]
                    + r1[g, 1, pl.ds(t, 1), :, lo:hi].astype(F32)
                    + r1[g, 2, pl.ds(t, 1), :, lo:hi].astype(F32)
                ).reshape(64, n)

            s2[g, 0, :, lo:hi] = summed(ring(sc[g], 2)).astype(BF16)
            send2(p, g, 0, 0, 0, second[g][0])
            send2(p, g, 1, 0, 32, second[g][1])
            s2[g, 1, :, lo:hi] = summed(ring(sc[g], 1)).astype(BF16)
            send2(p, g, 2, 1, 32, second[g][0])
            s2[g, 2, :, lo:hi] = summed(ring(sc[g], -1)).astype(BF16)
            send2(p, g, 3, 2, 0, second[g][1])
            own2[g, :, lo:hi] = summed(sc[g])

    def stage_u(p):
        lo, n = PIECES[p]
        hi = lo + n
        for g in range(2):
            for k in range(2):
                t = 32 * k
                slow[p][g][k].wait_recv()
                v = s2[g, 1 + k, t : t + 32, lo:hi].astype(F32) + r2[g, 0, t : t + 32, lo:hi].astype(F32)
                s2[g, 1 + k, t : t + 32, lo:hi] = v.astype(BF16)
                send2(p, g, 4 + k, 1 + k, t, second[g][k])

    def stage_v(p):
        lo, n = PIECES[p]
        hi = lo + n
        val = []
        for g in range(2):
            for i in (2, 3, 4, 5):
                slow[p][g][i].wait_recv()
            val.append(own2[g, :, lo:hi] + r2[g, 1, :, lo:hi].astype(F32) + r2[g, 2, :, lo:hi].astype(F32))
        if hi > COLS:
            lane = lax.broadcasted_iota(jnp.int32, (64, 128), 1)
            tail = val[0][:, n - 128 :] + val[1][:, n - 128 :]
            tot = jnp.sum(jnp.where(lane >= 112, tail, 0.0), axis=1, keepdims=True)
            rscale[...] = jnp.broadcast_to(lax.rsqrt(tot / D + EPSILON), (64, 128))
        scale = rscale[:, :1]
        gate, up = val[0] * scale, val[1] * scale
        hidden = (gate / (1.0 + jnp.exp(-gate)) * up).astype(BF16)
        m = min(n, COLS - lo)
        out_ref[:, lo : lo + m] = hidden[:, :m]

    def stage_cache(p):
        kv_copy[6].wait_recv()
        kv_copy[7].wait_recv()
        group = lax.broadcasted_iota(jnp.int32, (256, 64), 0) // 32
        hit = jnp.where(pages_ref[...] == r * 8 + group, 1.0, 0.0)
        has = jnp.sum(hit, axis=1, keepdims=True) > 0.5
        hit = hit.astype(BF16)
        slot = lax.broadcasted_iota(jnp.int32, (256, 512), 0)
        tok = lax.broadcasted_iota(jnp.int32, (256, 512), 1)
        src = lax.broadcasted_iota(jnp.int32, (64, 512), 0)
        dst = lax.broadcasted_iota(jnp.int32, (64, 512), 1) // 32
        new = jnp.zeros((256, 128), F32)
        for a in range(4):
            spread = jnp.where(src == a * 16 + dst, 1.0, 0.0).astype(BF16)
            pick = jnp.dot(hit, spread, preferred_element_type=F32)
            pick = jnp.where(slot % 32 == tok % 32, pick, 0.0).astype(BF16)
            new += jnp.dot(pick, kvb[a].reshape(512, 128), preferred_element_type=F32)
        old = cache_ref[...].astype(F32)
        cout_ref[...] = jnp.where(has & (new < 0.5 * DEAD), new, old).astype(BF16)

    for stage, p in (
        (stage_x, 0), (stage_x, 1), (stage_y, 0), (stage_x, 2), (stage_y, 1), (stage_z, 0),
        (stage_x, 3), (stage_y, 2), (stage_z, 1), (stage_u, 0), (stage_cache, 0), (stage_y, 3),
        (stage_z, 2), (stage_u, 1), (stage_v, 0), (stage_z, 3), (stage_u, 2), (stage_v, 1),
        (stage_u, 3), (stage_v, 2), (stage_v, 3),
    ):
        stage(p)
    for copy in started:
        copy.wait_send()


def layer(*args):
    vm = pl.BlockSpec(memory_space=pltpu.VMEM)
    hbm = pl.BlockSpec(memory_space=pl.ANY)
    dma = pltpu.SemaphoreType.DMA
    return pl.pallas_call(
        layer_kernel,
        out_shape=(
            jax.ShapeDtypeStruct((64, COLS), BF16),
            jax.ShapeDtypeStruct((256, 128), BF16),
        ),
        in_specs=[vm] * 6 + [hbm] * 3,
        out_specs=(vm, vm),
        scratch_shapes=[
            pltpu.VMEM((4, 4, 64, 512), BF16),
            pltpu.VMEM((1024, 512), BF16),
            pltpu.VMEM((2, 4, 4, 64, 512), BF16),
            pltpu.VMEM((4, 4, 128, 128), BF16),
            pltpu.VMEM((4, 256, 256), F32),
            pltpu.VMEM((4, 256, 256), BF16),
            pltpu.VMEM((4, 256, 256), BF16),
            pltpu.VMEM((4, 3, 64, 256), BF16),
            pltpu.VMEM((4, 3, 64, 256), BF16),
            pltpu.VMEM((4, 64, 256), F32),
            pltpu.VMEM((4, 2, 4, 64, 256), BF16),
            pltpu.VMEM((4, 4, 64, 512), BF16),
            pltpu.VMEM((2, WIDE, 512), BF16),
            pltpu.VMEM((4, 4, 64, 128), F32),
            pltpu.VMEM((2, 4, 64, 1024), F32),
            pltpu.VMEM((2, 64, WIDE), F32),
            pltpu.VMEM((64, 128), F32),
            pltpu.VMEM((2, 3, 4, 64, WIDE), BF16),
            pltpu.VMEM((2, 3, 4, 64, WIDE), BF16),
            pltpu.VMEM((2, 3, 64, WIDE), BF16),
            pltpu.VMEM((2, 3, 64, WIDE), BF16),
            dma((2,)),
            dma((4, 2)),
            dma((2, 5, 4)), dma((2, 5, 4)),
            dma((8,)), dma((8,)),
            dma((4,)), dma((4,)),
            dma((4, 10)), dma((4, 10)),
            dma((4,)), dma((4,)),
            dma((4, 2, 6)), dma((4, 2, 6)),
            dma((4, 2, 6)), dma((4, 2, 6)),
        ],
        compiler_params=pltpu.CompilerParams(collective_id=0, has_side_effects=True, vmem_limit_bytes=67043328),
        name="layer",
    )(*args)


def on_device(
    segments, queries, keys_values, page_table, paged_cache, residual, out_weight, norm_gain, gate_up_weight
):
    hidden, cache = layer(
        segments[None, :], page_table[None, :], norm_gain[None, :], queries, keys_values.reshape(128, 128),
        paged_cache.reshape(256, 128), residual.reshape(4, 4, 64, 512), out_weight,
        gate_up_weight.transpose(1, 2, 0),
    )
    return hidden, cache.reshape(8, 16, 2, 128)


def solution(mesh):
    placed = (
        P("req"),
        P("req", "mdl"),
        P("req", None, "mdl"),
        P(),
        P("req", None, None, "mdl"),
        P(None, "req"),
        P("mdl", "req"),
        P("req"),
        P("req", None, "mdl"),
    )
    return jax.shard_map(
        on_device,
        mesh=mesh,
        in_specs=placed,
        out_specs=(P("req", "mdl"), P("req", None, None, "mdl")),
        check_vma=False,
    )
```

time: 148 us -> 139 us (0.939)
  local copies, waits for them, and re-layouts: 9.08 us -> 4.6 us
  other arithmetic: 2.52 us -> 0 us
  Pallas kernels: 135 us -> 133 us
    pallas_call x2 -> x1, Pallas kernels: 135 us -> 133 us  [layer(): pl.pallas_call(layer_kernel, out_shape=(jax.ShapeDtypeStruct((64, COLS),...]
    reshape x2 -> x0, local copies, waits for them, and re-layouts: 2.18 us -> none  [the longest x1 1.49 us: on_device(): return (hidden, cache.reshape(8, 16, 2, 128))]
where the time goes in v2:
time: 139 us; the launch traced here: 138 us
  Pallas kernels  133 us (96%)
  local copies, waits for them, and re-layouts  4.6 us (3%)
    pallas_call x1, Pallas kernels, layer(): pl.pallas_call(layer_kernel, out_shape=(jax.ShapeDtypeStruct((64, COLS),...  133 us
    unnamed x2, local copies, waits for them, and re-layouts  3.34 us

profile of v2, /device:TPU:0, one launch (start us, length us, event | category | flops | bytes accessed | tf_op | source)
XLA Modules:
  0.0 137.9 jit_solution(2745887566540512292)
XLA Ops:
  0.6 1.3 broadcast_in_dim.11.gain_ref
  1.9 132.6 %layer.1 = (bf16[64,3696]{1,0:T(8,128)(2,1)}, bf16[256,128]{1,0:T(8,128)(2,1)}) custom-call(s32[1,64]{1,0:T(1,128)} %bitcast.12, s32[1,64]{1,0:T(1,128)} %bitcast.13, bf16[1,512]{1,0:T(2,128)(2,1)} %broadcast_in_dim.11.gain_ref, bf16[64,1024]{1,0:T(8,128)(2,1)} %q_ref.1, bf16[128,128]{1,0:T(8,128)(2,1)} %bitcast.11, bf16[256,128]{1,0:T(8,128)(2,1)} %bitcast.9, ...), custom_call_target="tpu_custom_call" | custom-call | tf_op jit(solution)/shard_map/layer/pallas_call | solution.py:470
  134.5 1.8 %copy.13 = bf16[64,3696]{1,0:T(8,128)(2,1)} copy(bf16[64,3696]{1,0:T(8,128)(2,1)} %get-tuple-element.8) | data formatting | bytes 946176
  136.4 1.5 %copy.14 = bf16[8,16,2,128]{3,2,1,0:T(2,128)(2,1)} copy(bf16[8,16,2,128]{3,2,1,0:T(2,128)(2,1)} %bitcast.10) | data formatting | bytes 131072

commit v3 on v2

--- a/solution.py
+++ b/solution.py
@@ -45,7 +45,15 @@
 
 WIDE = 3712
 COLS = 3696
-PIECES = ((2688, 1024), (0, 896), (896, 896), (1792, 896))
+QUART = 384
+SHARED = 4 * QUART
+PIECES = ((3072, 640), (1536, 768), (2304, 768))
+WIDEST = 768
+OWNED = WIDE - SHARED
+
+
+def quarter(q):
+    return pl.ds(pl.multiple_of(q * QUART, QUART), QUART)
 
 
 def layer_kernel(
@@ -53,8 +61,10 @@
     out_ref, cout_ref,
     res_ref, ow_ref, ag, kvb, acc_own, p2s, p2r, s2s, s2r, chunk_own, n2, ng_ref,
     w, ss, own1, own2, rscale, s1, r1, s2, r2,
+    wx, wt, nz, sw, rw, ownw, fs, fr, ft,
     in_sem, w_sem, ag_ss, ag_rs, kv_ss, kv_rs, p_ss, p_rs, x_ss, x_rs, n_ss, n_rs,
     ss1, rs1, ss2, rs2,
+    own_sem, wa_ss, wa_rs, nz_ss, nz_rs, xz_ss, xz_rs, sw_ss, sw_rs, fa_ss, fa_rs,
 ):
     y, z, x, c = position()
     zp, zm = dev(y, ring(z, 1), x, c), dev(y, ring(z, -1), x, c)
@@ -70,9 +80,12 @@
         for g in range(2):
             m = min(n, COLS - lo)
             loads.append(
-                pltpu.make_async_copy(w_ref.at[g, pl.ds(lo, m)], w.at[g, pl.ds(lo, m)], w_sem.at[p, g])
+                pltpu.make_async_copy(w_ref.at[g, pl.ds(lo, m)], w.at[g, pl.ds(lo - SHARED, m)], w_sem.at[p, g])
             )
             loads[-1].start()
+    for g, f in enumerate((z, y)):
+        loads.append(pltpu.make_async_copy(w_ref.at[g, quarter(f)], wx.at[g, f], own_sem.at[g]))
+        loads[-1].start()
     started = []
 
     def go(copy):
@@ -259,6 +272,98 @@
             v = v.reshape(256, 256).astype(F32) * ginv[:, at]
             squares += jnp.sum(v * v, axis=1, keepdims=True)
         ss[ya] = jnp.broadcast_to(squares, (256, 128)).reshape(4, 64, 128)
+
+    def swap_start(g, src, dst, far, far_dst, ss_, rs_):
+        f = fc[g]
+        plus, minus = first[g]
+        return [
+            go(copy_to(src(ring(f, 1)), dst(f), ss_.at[g, 0], rs_.at[g, 0], plus)),
+            go(copy_to(src(ring(f, -1)), dst(f), ss_.at[g, 1], rs_.at[g, 1], minus)),
+            go(copy_to(far(0), far_dst(0), ss_.at[g, 2], rs_.at[g, 2], plus)),
+            go(copy_to(far(1), far_dst(1), ss_.at[g, 3], rs_.at[g, 3], minus)),
+        ]
+
+    def swap_relay(g, copies, held, dst, ss_, rs_):
+        f = fc[g]
+        plus, minus = first[g]
+        copies[2].wait_recv()
+        copies.append(go(copy_to(held(0), dst(ring(f, -1), 0), ss_.at[g, 4], rs_.at[g, 4], plus)))
+        copies[3].wait_recv()
+        copies.append(go(copy_to(held(1), dst(ring(f, 1), 1), ss_.at[g, 5], rs_.at[g, 5], minus)))
+
+    def swap_finish(copies):
+        for i in (0, 1, 4, 5):
+            copies[i].wait_recv()
+
+    weights = [None] * 2
+    half_q = QUART // 2
+
+    def weights_start():
+        for g in range(2):
+
+            def far(k, g=g):
+                at = ring(fc[g], 2) * QUART + k * half_q
+                return w_ref.at[g, pl.ds(pl.multiple_of(at, half_q), half_q)]
+
+            weights[g] = swap_start(
+                g, lambda q: w_ref.at[g, quarter(q)], lambda p: wx.at[g, p],
+                far, lambda k: wt.at[g, k], wa_ss, wa_rs,
+            )
+
+    def weights_relay():
+        for g in range(2):
+            swap_relay(
+                g, weights[g], lambda k: wt.at[g, k],
+                lambda p, k: wx.at[g, p, pl.ds(k * half_q, half_q)], wa_ss, wa_rs,
+            )
+
+    rows_copy = [[None] * 4 for _ in range(2)]
+    side = [[[None] * 5 for _ in range(3)] for _ in range(2)]
+    every = slice(None)
+
+    def rows_start():
+        for g in range(2):
+            for k in range(2):
+                rows_copy[g][k] = go(copy_to(
+                    n2.at[every, c, x], nz.at[g, k, every, c, x], nz_ss.at[g, k], nz_rs.at[g, k], first[g][k]
+                ))
+
+    def rows_relay():
+        for g in range(2):
+            for k in range(2):
+                rows_copy[g][k].wait_recv()
+                at = pl.ds(2 * k, 2)
+                rows_copy[g][2 + k] = go(copy_to(
+                    nz.at[g, k, at, c, x], nz.at[g, 2, at, c, x], nz_ss.at[g, 2 + k], nz_rs.at[g, 2 + k], first[g][k]
+                ))
+
+    def side_msg(g, j, i, ref, peer):
+        side[g][j][i] = go(copy_to(ref, ref, xz_ss.at[g, j, i], xz_rs.at[g, j, i], peer))
+
+    def side_start(j):
+        for g in range(2):
+            if j == 2:
+                rows_copy[g][2].wait_recv()
+                rows_copy[g][3].wait_recv()
+            side_msg(g, j, 0, nz.at[g, j, every, c, x], xp)
+            side_msg(g, j, 1, nz.at[g, j, every, c, x], xm)
+
+    def side_relay(j):
+        for g in range(2):
+            side[g][j][0].wait_recv()
+            side_msg(g, j, 2, nz.at[g, j, pl.ds(0, 2), c, ring(x, -1)], xp)
+            side[g][j][1].wait_recv()
+            side_msg(g, j, 3, nz.at[g, j, pl.ds(2, 2), c, ring(x, 1)], xm)
+
+    def side_pair(j):
+        for g in range(2):
+            side[g][j][2].wait_recv()
+            side[g][j][3].wait_recv()
+            side_msg(g, j, 4, nz.at[g, j, every, c], partner)
+
+    def side_finish(j):
+        for g in range(2):
+            side[g][j][4].wait_recv()
 
     for half in range(2):
         start_one(half)
@@ -283,6 +388,7 @@
     reduce_a(0)
     for half in range(2):
         forward_two(half, 3)
+    weights_start()
     finish_two(1, 1)
     project(1)
     reduce_b(0)
@@ -314,9 +420,11 @@
     reduce_e(2)
     reduce_f(1)
     kv_rows_forward()
+    rows_start()
     reduce_d(3)
     reduce_f(2)
     reduce_e(3)
+    weights_relay()
     reduce_f(3)
 
     r = lax.axis_index("req")
@@ -327,7 +435,8 @@
 
     def partial(g, d, p):
         lo, n = PIECES[p]
-        out = lax.dot_general(rows_of(ng_ref, g, d, 512), w[g, lo : lo + n], NT, preferred_element_type=F32)
+        at = slice(lo - SHARED, lo - SHARED + n)
+        out = lax.dot_general(rows_of(ng_ref, g, d, 512), w[g, at], NT, preferred_element_type=F32)
         if lo + n > COLS:
             tot = rows_of(ss, g, d, 128)
             high = tot.astype(BF16).astype(F32)
@@ -338,21 +447,25 @@
             out = jnp.concatenate([out[:, : n - 128], tail], axis=1)
         return out.reshape(4, 64, n)
 
-    fast = [[[None] * 6 for _ in range(2)] for _ in range(4)]
-    slow = [[[None] * 6 for _ in range(2)] for _ in range(4)]
+    fast = [[[None] * 6 for _ in range(2)] for _ in range(3)]
+    slow = [[[None] * 6 for _ in range(2)] for _ in range(3)]
 
     def send1(p, g, i, k, t, peer):
         lo, n = PIECES[p]
-        at = (g, k, pl.ds(t, 2), slice(None), pl.ds(lo, n))
+        at = (g, k, pl.ds(t, 2), slice(None), pl.ds(lo - SHARED, n))
         fast[p][g][i] = go(copy_to(s1.at[at], r1.at[at], ss1.at[p, g, i], rs1.at[p, g, i], peer))
 
     def send2(p, g, i, k, t, peer):
         lo, n = PIECES[p]
-        at = (g, k, pl.ds(t, 32), pl.ds(lo, n))
+        at = (g, k, pl.ds(t, 32), pl.ds(lo - SHARED, n))
         slow[p][g][i] = go(copy_to(s2.at[at], r2.at[at], ss2.at[p, g, i], rs2.at[p, g, i], peer))
+
+    def swiglu(gate, up):
+        return (gate / (1.0 + jnp.exp(-gate)) * up).astype(BF16)
 
     def stage_x(p):
         lo, n = PIECES[p]
+        lo -= SHARED
         hi = lo + n
         for g in range(2):
             loads[2 * p + g].wait()
@@ -367,6 +480,7 @@
 
     def stage_y(p):
         lo, n = PIECES[p]
+        lo -= SHARED
         hi = lo + n
         for g in range(2):
             for k in range(2):
@@ -378,6 +492,7 @@
 
     def stage_z(p):
         lo, n = PIECES[p]
+        lo -= SHARED
         hi = lo + n
         for g in range(2):
             own1[g, :, :, :n] = partial(g, fc[g], p)
@@ -404,6 +519,7 @@
 
     def stage_u(p):
         lo, n = PIECES[p]
+        lo -= SHARED
         hi = lo + n
         for g in range(2):
             for k in range(2):
@@ -415,22 +531,95 @@
 
     def stage_v(p):
         lo, n = PIECES[p]
+        lo -= SHARED
         hi = lo + n
         val = []
         for g in range(2):
             for i in (2, 3, 4, 5):
                 slow[p][g][i].wait_recv()
             val.append(own2[g, :, lo:hi] + r2[g, 1, :, lo:hi].astype(F32) + r2[g, 2, :, lo:hi].astype(F32))
-        if hi > COLS:
+        if hi > COLS - SHARED:
             lane = lax.broadcasted_iota(jnp.int32, (64, 128), 1)
             tail = val[0][:, n - 128 :] + val[1][:, n - 128 :]
             tot = jnp.sum(jnp.where(lane >= 112, tail, 0.0), axis=1, keepdims=True)
             rscale[...] = jnp.broadcast_to(lax.rsqrt(tot / D + EPSILON), (64, 128))
         scale = rscale[:, :1]
-        gate, up = val[0] * scale, val[1] * scale
-        hidden = (gate / (1.0 + jnp.exp(-gate)) * up).astype(BF16)
-        m = min(n, COLS - lo)
-        out_ref[:, lo : lo + m] = hidden[:, :m]
+        hidden = swiglu(val[0] * scale, val[1] * scale)
+        m = min(n, COLS - SHARED - lo)
+        out_ref[:, SHARED + lo : SHARED + lo + m] = hidden[:, :m]
+
+    ring_w = [[None] * 6 for _ in range(2)]
+    back_w = [None] * 2
+
+    def shared_partial(g, d):
+        out = 0.0
+        for j, off in ((None, 0), (0, -1), (1, 1), (2, 2)):
+            p = ring(fc[g], off)
+            for h in range(2):
+                if g == 0:
+                    v = n2[pl.ds(d, 1), h] if j is None else nz[g, j, pl.ds(d, 1), h]
+                else:
+                    v = n2[:, h, pl.ds(d, 1)] if j is None else nz[g, j, :, h, pl.ds(d, 1)]
+                u = wx[g, pl.ds(p, 1), :, h * 256 : h * 256 + 256].reshape(QUART, 256)
+                out += lax.dot_general(v.reshape(256, 256), u, NT, preferred_element_type=F32)
+        return out.reshape(4, 64, QUART)
+
+    def send_w(g, i, k, t, peer):
+        at = (g, k, pl.ds(t, 2))
+        ring_w[g][i] = go(copy_to(sw.at[at], rw.at[at], sw_ss.at[g, i], sw_rs.at[g, i], peer))
+
+    def shared_x(p):
+        for g in range(2):
+            swap_finish(weights[g])
+            loads[2 * len(PIECES) + g].wait()
+            sw[g, 0] = shared_partial(g, ring(sc[g], 2)).astype(BF16)
+            send_w(g, 0, 0, 0, second[g][0])
+            send_w(g, 1, 0, 2, second[g][1])
+        for g in range(2):
+            sw[g, 1] = shared_partial(g, ring(sc[g], 1)).astype(BF16)
+            send_w(g, 2, 1, 2, second[g][0])
+            sw[g, 2] = shared_partial(g, ring(sc[g], -1)).astype(BF16)
+            send_w(g, 3, 2, 0, second[g][1])
+
+    def shared_y(p):
+        for g in range(2):
+            for k in range(2):
+                t = 2 * k
+                ring_w[g][k].wait_recv()
+                v = sw[g, 1 + k, t : t + 2].astype(F32) + rw[g, 0, t : t + 2].astype(F32)
+                sw[g, 1 + k, t : t + 2] = v.astype(BF16)
+                send_w(g, 4 + k, 1 + k, t, second[g][k])
+
+    def shared_own(p):
+        for g in range(2):
+            ownw[g] = shared_partial(g, sc[g])
+
+    def shared_z(p):
+        for g in range(2):
+            for i in (2, 3, 4, 5):
+                ring_w[g][i].wait_recv()
+            fs[g] = (ownw[g] + rw[g, 1].astype(F32) + rw[g, 2].astype(F32)).astype(BF16)
+            fr[g, pl.ds(fc[g], 1)] = fs[g, pl.ds(fc[g], 1)]
+            back_w[g] = swap_start(
+                g, lambda q: fs.at[g, q], lambda q: fr.at[g, q],
+                lambda k: fs.at[g, ring(fc[g], 2), pl.ds(32 * k, 32)], lambda k: ft.at[g, k], fa_ss, fa_rs,
+            )
+
+    def shared_u(p):
+        for g in range(2):
+            swap_relay(
+                g, back_w[g], lambda k: ft.at[g, k],
+                lambda q, k: fr.at[g, q, pl.ds(32 * k, 32)], fa_ss, fa_rs,
+            )
+
+    def shared_v(p):
+        for g in range(2):
+            swap_finish(back_w[g])
+        scale = rscale[:, :1]
+        for q in range(4):
+            out_ref[:, q * QUART : (q + 1) * QUART] = swiglu(
+                fr[0, q].astype(F32) * scale, fr[1, q].astype(F32) * scale
+            )
 
     def stage_cache(p):
         kv_copy[6].wait_recv()
@@ -452,11 +641,25 @@
         old = cache_ref[...].astype(F32)
         cout_ref[...] = jnp.where(has & (new < 0.5 * DEAD), new, old).astype(BF16)
 
+    def rows_on(p):
+        if p < 3:
+            side_start(p)
+        elif p < 6:
+            side_relay(p - 3)
+        elif p < 9:
+            side_pair(p - 6)
+        elif p < 12:
+            side_finish(p - 9)
+        else:
+            rows_relay()
+
     for stage, p in (
-        (stage_x, 0), (stage_x, 1), (stage_y, 0), (stage_x, 2), (stage_y, 1), (stage_z, 0),
-        (stage_x, 3), (stage_y, 2), (stage_z, 1), (stage_u, 0), (stage_cache, 0), (stage_y, 3),
-        (stage_z, 2), (stage_u, 1), (stage_v, 0), (stage_z, 3), (stage_u, 2), (stage_v, 1),
-        (stage_u, 3), (stage_v, 2), (stage_v, 3),
+        (stage_x, 0), (rows_on, 12), (rows_on, 0), (rows_on, 1), (stage_x, 1), (stage_y, 0),
+        (rows_on, 2), (rows_on, 3), (stage_x, 2), (rows_on, 4), (stage_y, 1), (stage_z, 0),
+        (rows_on, 5), (rows_on, 6), (rows_on, 7), (stage_y, 2), (stage_z, 1), (rows_on, 8),
+        (rows_on, 9), (rows_on, 10), (stage_u, 0), (rows_on, 11), (shared_x, 0), (stage_u, 1),
+        (stage_z, 2), (stage_v, 0), (shared_y, 0), (stage_cache, 0), (shared_own, 0), (stage_u, 2),
+        (stage_v, 1), (shared_z, 0), (stage_v, 2), (shared_u, 0), (shared_v, 0),
     ):
         stage(p)
     for copy in started:
@@ -488,24 +691,39 @@
             pltpu.VMEM((4, 64, 256), F32),
             pltpu.VMEM((4, 2, 4, 64, 256), BF16),
             pltpu.VMEM((4, 4, 64, 512), BF16),
-            pltpu.VMEM((2, WIDE, 512), BF16),
+            pltpu.VMEM((2, OWNED, 512), BF16),
             pltpu.VMEM((4, 4, 64, 128), F32),
-            pltpu.VMEM((2, 4, 64, 1024), F32),
-            pltpu.VMEM((2, 64, WIDE), F32),
+            pltpu.VMEM((2, 4, 64, WIDEST), F32),
+            pltpu.VMEM((2, 64, OWNED), F32),
             pltpu.VMEM((64, 128), F32),
-            pltpu.VMEM((2, 3, 4, 64, WIDE), BF16),
-            pltpu.VMEM((2, 3, 4, 64, WIDE), BF16),
-            pltpu.VMEM((2, 3, 64, WIDE), BF16),
-            pltpu.VMEM((2, 3, 64, WIDE), BF16),
+            pltpu.VMEM((2, 3, 4, 64, OWNED), BF16),
+            pltpu.VMEM((2, 3, 4, 64, OWNED), BF16),
+            pltpu.VMEM((2, 3, 64, OWNED), BF16),
+            pltpu.VMEM((2, 3, 64, OWNED), BF16),
+            pltpu.VMEM((2, 4, QUART, 512), BF16),
+            pltpu.VMEM((2, 2, QUART // 2, 512), BF16),
+            pltpu.VMEM((2, 3, 4, 2, 4, 64, 256), BF16),
+            pltpu.VMEM((2, 3, 4, 64, QUART), BF16),
+            pltpu.VMEM((2, 3, 4, 64, QUART), BF16),
+            pltpu.VMEM((2, 4, 64, QUART), F32),
+            pltpu.VMEM((2, 4, 64, QUART), BF16),
+            pltpu.VMEM((2, 4, 64, QUART), BF16),
+            pltpu.VMEM((2, 2, 32, QUART), BF16),
             dma((2,)),
-            dma((4, 2)),
+            dma((3, 2)),
             dma((2, 5, 4)), dma((2, 5, 4)),
             dma((8,)), dma((8,)),
             dma((4,)), dma((4,)),
             dma((4, 10)), dma((4, 10)),
             dma((4,)), dma((4,)),
-            dma((4, 2, 6)), dma((4, 2, 6)),
-            dma((4, 2, 6)), dma((4, 2, 6)),
+            dma((3, 2, 6)), dma((3, 2, 6)),
+            dma((3, 2, 6)), dma((3, 2, 6)),
+            dma((2,)),
+            dma((2, 6)), dma((2, 6)),
+            dma((2, 4)), dma((2, 4)),
+            dma((2, 3, 5)), dma((2, 3, 5)),
+            dma((2, 6)), dma((2, 6)),
+            dma((2, 6)), dma((2, 6)),
         ],
         compiler_params=pltpu.CompilerParams(collective_id=0, has_side_effects=True, vmem_limit_bytes=67043328),
         name="layer",

time: 139 us -> 131 us (0.942)
  Pallas kernels: 133 us -> 125 us
    pallas_call x1, Pallas kernels: 133 us -> 125 us  [layer(): pl.pallas_call(layer_kernel, out_shape=(jax.ShapeDtypeStruct((64, COLS),...]
where the time goes in v3:
time: 131 us; the launch traced here: 130 us
  Pallas kernels  125 us (95%)
  local copies, waits for them, and re-layouts  4.6 us (4%)
    pallas_call x1, Pallas kernels, layer(): pl.pallas_call(layer_kernel, out_shape=(jax.ShapeDtypeStruct((64, COLS),...  125 us
    unnamed x2, local copies, waits for them, and re-layouts  3.34 us

profile of v3, /device:TPU:0, one launch (start us, length us, event | category | flops | bytes accessed | tf_op | source)
XLA Modules:
  0.0 130.5 jit_solution(8336272406094201027)
XLA Ops:
  0.6 1.3 broadcast_in_dim.11.gain_ref
  1.9 125.2 %layer.1 = (bf16[64,3696]{1,0:T(8,128)(2,1)}, bf16[256,128]{1,0:T(8,128)(2,1)}) custom-call(s32[1,64]{1,0:T(1,128)} %bitcast.12, s32[1,64]{1,0:T(1,128)} %bitcast.13, bf16[1,512]{1,0:T(2,128)(2,1)} %broadcast_in_dim.11.gain_ref, bf16[64,1024]{1,0:T(8,128)(2,1)} %q_ref.1, bf16[128,128]{1,0:T(8,128)(2,1)} %bitcast.11, bf16[256,128]{1,0:T(8,128)(2,1)} %bitcast.9, ...), custom_call_target="tpu_custom_call" | custom-call | tf_op jit(solution)/shard_map/layer/pallas_call | solution.py:673
  127.1 1.8 %copy.13 = bf16[64,3696]{1,0:T(8,128)(2,1)} copy(bf16[64,3696]{1,0:T(8,128)(2,1)} %get-tuple-element.8) | data formatting | bytes 946176
  129.0 1.5 %copy.14 = bf16[8,16,2,128]{3,2,1,0:T(2,128)(2,1)} copy(bf16[8,16,2,128]{3,2,1,0:T(2,128)(2,1)} %bitcast.10) | data formatting | bytes 131072
